TPU v7x, 512 devices: a whole 4x4x16 slice. The times are simulated.
512 devices in a mesh: mem: 16 (over z), sp: 32 (over x, y, core).
Axes of the slice: x: 4, y: 4, z: 16, core: 2. Of those that a mesh axis runs over, the one named last changes fastest.
Arguments:
- ensemble: bfloat16 [256, 131072], P('mem', 'sp'), may hold values from -6 to 6
- predicted: bfloat16 [256, 65536], P('mem', 'sp'), may hold values from -2 to 2
- observed: float32 [65536], P('sp'), may hold values from -6 to 6
- perturbation: bfloat16 [256, 65536], P('mem', 'sp'), may hold values from -6 to 6
- noise_variance: float32 [512], P('sp'), may hold values from 0.25 to 4
- block_lists: int32 [32, 64], P('sp'), may hold values from 0 to 511, as said below
- localization: int32 [1024, 64], P('sp'), may hold values 0 or 1
Outputs:
- increment: float32 [256, 131072], P('mem', 'sp')
Inputs may be any that keep to these rules, and one draw needn't show every extreme that they name: `block_lists`: row t lists the 64 distinct data blocks used by the bricks of index t of sp, in increasing order; block j is held by index j // 16; a row uses 1 to 3 blocks of each holder, exactly 3 of some holder, and every holder gives 3 blocks to some row.
All inputs are finite; a program needn't handle non-finite values. No bound on the sum of `localization` on one device may be relied on, other than what follows from the above.
Results may differ from a plain program's by a relative error of at most 0.0055.
Values may be sent and summed in bfloat16 or wider, within the bound.
No kernel may reach another device: no remote copies, remote signals or barrier semaphores. Data moves between devices by JAX's collectives and lax.ppermute only.
A program may use at most 64 MiB of HBM per device.

v0:
```python
import jax
import jax.numpy as jnp
from jax import lax
from jax.sharding import PartitionSpec as P

SLOTS = 3


def per_device(
    ensemble, predicted, observed, perturbation, noise_variance, block_lists, localization
):
    bf16, f32 = (jnp.bfloat16, jnp.float32)
    mem, sp = (lax.axis_size("mem"), lax.axis_size("sp"))
    local = ensemble.shape[0]
    members = local * mem
    cells = ensemble.shape[1]
    bricks = localization.shape[0]
    brick = cells // bricks
    blocks = noise_variance.shape[0]
    block = predicted.shape[1] // blocks
    need = block_lists.shape[1]
    whole_ensemble = lax.all_gather(ensemble, "mem", axis=0, tiled=True)
    needed = block_lists[0]
    holder = needed // blocks
    before = jnp.sum(needed[None, :] < (holder * blocks)[:, None], axis=1)
    slot = holder * SLOTS + (jnp.arange(need) - before)
    slot_hot = slot[:, None] == jnp.arange(sp * SLOTS)[None, :]
    asked = jnp.sum(jnp.where(slot_hot, (needed % blocks)[:, None], 0), axis=0)
    asked = jnp.pad(asked.reshape(sp, SLOTS), ((0, 0), (0, 128 - SLOTS)))
    wanted = lax.all_to_all(asked, "sp", split_axis=0, concat_axis=0, tiled=True)
    wanted = wanted[:, :SLOTS].reshape(-1)
    slot_pattern = jnp.dot(
        localization.astype(bf16), slot_hot.astype(bf16), preferred_element_type=f32
    ).astype(bf16)
    cut = (blocks - 1) * block
    last = jnp.broadcast_to(predicted[None, :, cut:], (mem, local, block))
    last = lax.all_to_all(last, "mem", split_axis=0, concat_axis=0, tiled=True)
    first, wanted = lax.optimization_barrier((predicted[:, :cut], wanted))
    first = lax.all_gather(first, "mem", axis=0, tiled=True)
    whole_predicted = jnp.concatenate([first, last.reshape(members, block)], axis=1)
    data_mean = jnp.sum(whole_predicted, axis=0, dtype=f32) / members
    data_anomalies = (whole_predicted.astype(f32) - data_mean).astype(bf16)
    variance = jnp.repeat(noise_variance, block)
    innovation = (
        observed[None, :] + jnp.sqrt(variance) * perturbation.astype(f32) - predicted.astype(f32)
    )
    weighted = (innovation / variance).astype(bf16)
    products = jnp.einsum(
        "njd,mjd->jnm",
        weighted.reshape(local, blocks, block),
        data_anomalies.reshape(members, blocks, block),
        preferred_element_type=f32,
    ).astype(bf16)
    picked = (wanted[:, None] == jnp.arange(blocks)[None, :]).astype(bf16)
    sent = jnp.einsum("sj,jnm->snm", picked, products, preferred_element_type=f32).astype(bf16)
    sent = sent.reshape(sp, SLOTS * local, members)
    got = lax.all_to_all(sent, "sp", split_axis=0, concat_axis=0, tiled=True)
    got = got.reshape(sp * SLOTS, local, members)
    gains = jnp.einsum("bs,snm->bnm", slot_pattern, got, preferred_element_type=f32).astype(bf16)
    model_mean = jnp.sum(whole_ensemble, axis=0, dtype=f32) / members
    model_anomalies = (whole_ensemble.astype(f32) - model_mean).astype(bf16)
    increment = jnp.einsum(
        "bnm,mbc->nbc",
        gains,
        model_anomalies.reshape(members, bricks, brick),
        preferred_element_type=f32,
    )
    return increment.reshape(local, cells) / (members - 1)


def solution(mesh):
    in_specs = (
        P("mem", "sp"),
        P("mem", "sp"),
        P("sp"),
        P("mem", "sp"),
        P("sp"),
        P("sp", None),
        P("sp", None),
    )
    return jax.shard_map(
        per_device, mesh=mesh, in_specs=in_specs, out_specs=P("mem", "sp"), check_vma=False
    )
```

profile of v0, /device:TPU:1, one launch (start us, length us, event | category | flops | bytes accessed | tf_op | source)
XLA Modules:
  0.0 114.8 jit_solution(8211245117296514880)
XLA Ops:
  6.5 0.0 copy-start.1
  6.5 0.0 copy-start.3
  6.5 0.0 copy-start.4
  6.5 0.0 all-gather.2.cloned.1.call-start
  6.5 0.7 all-gather.2.cloned.1.call-update
  7.3 0.7 broadcast_multiply_fusion.1
  7.9 0.8 convert_reduce_fusion.2
  8.8 0.1 select_reduce_fusion
  8.9 0.1 reshape.124
  9.0 0.6 pad.4
  9.6 10.4 %all-to-all-start = ((s32[32,1,128]{2,1,0:T(1,128)}), s32[32,1,128]{2,1,0:T(1,128)S(1)}, u32[]{:S(2)}, u32[]{:S(2)}) async-start(s32[32,1,128]{2,1,0:T(1,128)} %bitcast.3), calls=%async_computation | async-start | bytes 32768 | tf_op jit(solution)/shard_map/all_to_all | solution.py:30
  20.0 0.7 bitcast_sqrt_fusion
  20.7 0.7 broadcast_bitcast_fusion
  21.4 0.8 slice.9
  22.3 0.7 slice.11
  23.0 4.0 %all-to-all-done = s32[32,1,128]{2,1,0:T(1,128)S(1)} async-done(((s32[32,1,128]{2,1,0:T(1,128)}), s32[32,1,128]{2,1,0:T(1,128)S(1)}, u32[]{:S(2)}, u32[]{:S(2)}) %all-to-all-start) | async-done | bytes 16416 | tf_op jit(solution)/shard_map/all_to_all | solution.py:30
  27.0 0.6 broadcast_in_dim.19
  27.6 13.0 %all-to-all-start.1 = ((bf16[16,16,128]{2,1,0:T(8,128)(2,1)}), bf16[16,16,128]{2,1,0:T(8,128)(2,1)S(1)}, u32[]{:S(2)}, u32[]{:S(2)}) async-start(bf16[16,16,128]{2,1,0:T(8,128)(2,1)} %broadcast_in_dim.19), calls=%async_computation.1 | async-start | bytes 131072 | tf_op jit(solution)/shard_map/all_to_all | solution.py:37
  40.6 0.1 reshape.125
  40.7 40.6 %all_gather.7 = bf16[256,1920]{1,0:T(8,128)(2,1)S(1)} all-gather(bf16[16,1920]{1,0:T(8,128)(2,1)S(1)} %slice.9), channel_id=1, replica_groups=mesh['mem'=16,'sp'=32] {'mem'}, dimensions={0}, use_global_device_ids=true | all-gather | bytes 1044480 | tf_op jit(solution)/shard_map/all_gather | solution.py:39
  81.4 0.0 all-to-all-done.1
  81.4 0.2 convert_reduce_fusion.1
  81.5 0.0 copy-done.1
  81.5 0.0 copy-done.3
  81.6 0.0 copy-done.4
  81.6 0.4 convolution_convert_fusion.2
  82.0 0.0 copy-start.2
  82.0 0.4 convolution_convert_fusion
  82.4 0.4 copy.33
  82.8 21.2 %all_to_all.22 = bf16[32,48,256]{2,1,0:T(8,128)(2,1)S(1)} all-to-all(bf16[32,48,256]{2,1,0:T(8,128)(2,1)S(1)} %bitcast.61), channel_id=1, replica_groups=mesh['mem'=16,'sp'=32] {'sp'}, dimensions={0} | all-to-all | bytes 1572864 | tf_op jit(solution)/shard_map/all_to_all | solution.py:57
  104.0 0.0 copy-done.2
  104.0 0.4 convolution_convert_fusion.1
  104.5 0.0 all-gather.2.cloned.1.call-done
  104.5 0.0 copy-start
  104.5 2.1 %convert_reduce_fusion = f32[4096]{0:T(1024)S(1)} fusion(bf16[256,4096]{1,0:T(8,128)(2,1)} %all-gather.2.cloned.1.call-done), kind=kLoop, calls=%fused_computation.1 | loop fusion | flops 2093056 | bytes 2113536 | tf_op jit(solution)/shard_map/reduce_sum | solution.py:60
  106.6 0.1 copy-done
  106.7 0.6 fusion.9
  107.3 0.7 copy.63
  (3 shorter events, 0.0 us)
Async XLA Ops:
  6.5 75.0 %copy-start.1 = (bf16[16,2048]{1,0:T(8,128)(2,1)S(1)}, bf16[16,2048]{1,0:T(8,128)(2,1)}, u32[]{:S(2)}) copy-start(bf16[16,2048]{1,0:T(8,128)(2,1)} %param.8) | copy-start | bytes 196612
  6.5 75.0 %copy-start.3 = (bf16[16,2048]{1,0:T(8,128)(2,1)S(1)}, bf16[16,2048]{1,0:T(8,128)(2,1)}, u32[]{:S(2)}) copy-start(bf16[16,2048]{1,0:T(8,128)(2,1)} %param.10) | copy-start | bytes 196612
  6.5 75.0 %copy-start.4 = (f32[2048]{0:T(1024)S(1)}, f32[2048]{0:T(1024)}, u32[]{:S(2)}) copy-start(f32[2048]{0:T(1024)} %param.9) | copy-start | bytes 24580
  6.5 97.9 %all-gather.2.cloned.1.call-start = ((), (), s32[]{:S(2)}) async-start(), calls=%async_computation.3 | async-start | bytes 2228224 | tf_op jit(solution)/shard_map/all_gather | solution.py:22
  9.6 17.3 %all-to-all-start = ((s32[32,1,128]{2,1,0:T(1,128)}), s32[32,1,128]{2,1,0:T(1,128)S(1)}, u32[]{:S(2)}, u32[]{:S(2)}) async-start(s32[32,1,128]{2,1,0:T(1,128)} %bitcast.3), calls=%async_computation | async-start | bytes 32768 | tf_op jit(solution)/shard_map/all_to_all | solution.py:30
  27.6 53.8 %all-to-all-start.1 = ((bf16[16,16,128]{2,1,0:T(8,128)(2,1)}), bf16[16,16,128]{2,1,0:T(8,128)(2,1)S(1)}, u32[]{:S(2)}, u32[]{:S(2)}) async-start(bf16[16,16,128]{2,1,0:T(8,128)(2,1)} %broadcast_in_dim.19), calls=%async_computation.1 | async-start | bytes 131072 | tf_op jit(solution)/shard_map/all_to_all | solution.py:37
  82.0 22.1 %copy-start.2 = (s32[32,64]{1,0:T(8,128)S(1)}, s32[32,64]{1,0:T(8,128)}, u32[]{:S(2)}) copy-start(s32[32,64]{1,0:T(8,128)} %param.13) | copy-start | bytes 24580
  104.5 2.2 %copy-start = (bf16[256,4096]{1,0:T(8,128)(2,1)S(1)}, bf16[256,4096]{1,0:T(8,128)(2,1)}, u32[]{:S(2)}) copy-start(bf16[256,4096]{1,0:T(8,128)(2,1)} %all-gather.2.cloned.1.call-done) | copy-start | bytes 6291460
Sparse Core Ops, SparseCore 0:
  9.4 73.4 all-gather.1
where the time goes:
time: 115 us
  blocking collectives  61.8 us (54%)
  starting transfers between devices  23.4 us (20%)
  between operations  13.5 us (12%)
  local copies, waits for them, and re-layouts  5.73 us (5%)
  waiting for transfers between devices  4.72 us (4%)
  other arithmetic  3.88 us (3%)
  matrix products  1.82 us (2%)
    all_gather x1, blocking collectives, per_device(): first = lax.all_gather(first, 'mem', axis=0, tiled=True)  40.6 us
    all_to_all x1, blocking collectives, per_device(): got = lax.all_to_all(sent, 'sp', split_axis=0, concat_axis=0, tiled=True)  21.2 us
    all_to_all x1, starting transfers between devices, per_device(): last = lax.all_to_all(last, 'mem', split_axis=0, concat_axis=0, tiled=True)  13 us
    all_to_all x1, starting transfers between devices, per_device(): lax.all_to_all(asked, 'sp', split_axis=0, concat_axis=0, tiled=True)  10.4 us
    all_to_all x1, waiting for transfers between devices, per_device(): lax.all_to_all(asked, 'sp', split_axis=0, concat_axis=0, tiled=True)  4 us
  transfers between devices with their start and end apart: 3, of which 1 were waited for; matrix products, arithmetic and copies ran while one was open for 7% of the time, Pallas kernels for 0%

commit v1 on v0

--- a/solution.py
+++ b/solution.py
@@ -4,6 +4,16 @@
 from jax.sharding import PartitionSpec as P
 
 SLOTS = 3
+
+
+def numbers_perform(view, array_axis):
+    made = []
+    for _ in range(lax.axis_size("mem")):
+        made.append(view)
+    r2 = jnp.concatenate(
+        lax.all_to_all(jnp.stack(made, 0), axis_name="mem", concat_axis=0, split_axis=0), array_axis
+    )
+    return r2
 
 
 def per_device(
@@ -36,7 +46,7 @@
     last = jnp.broadcast_to(predicted[None, :, cut:], (mem, local, block))
     last = lax.all_to_all(last, "mem", split_axis=0, concat_axis=0, tiled=True)
     first, wanted = lax.optimization_barrier((predicted[:, :cut], wanted))
-    first = lax.all_gather(first, "mem", axis=0, tiled=True)
+    first = numbers_perform(first, 0)
     whole_predicted = jnp.concatenate([first, last.reshape(members, block)], axis=1)
     data_mean = jnp.sum(whole_predicted, axis=0, dtype=f32) / members
     data_anomalies = (whole_predicted.astype(f32) - data_mean).astype(bf16)

time: 115 us -> 158 us (1.37)
  the two profiles are of different devices: /device:TPU:1 before, /device:TPU:2 now
where the time goes in v1:
time: 158 us; the launch traced here: 157 us
  waiting for transfers between devices  96 us (61%)
  starting transfers between devices  32 us (20%)
  between operations  13.5 us (9%)
  local copies, waits for them, and re-layouts  8.22 us (5%)
  other arithmetic  5.44 us (3%)
  matrix products  1.88 us (1%)
    all_to_all x1, waiting for transfers between devices, numbers_perform(): lax.all_to_all(jnp.stack(made, 0), axis_name='mem', concat_axis=0, split_...  50.8 us
    all_gather x1, waiting for transfers between devices, per_device(): whole_ensemble = lax.all_gather(ensemble, 'mem', axis=0, tiled=True)  27.3 us
    all_to_all x1, starting transfers between devices, per_device(): last = lax.all_to_all(last, 'mem', split_axis=0, concat_axis=0, tiled=True)  13.3 us
    all_to_all x1, waiting for transfers between devices, per_device(): last = lax.all_to_all(last, 'mem', split_axis=0, concat_axis=0, tiled=True)  11.7 us
    all_to_all x1, starting transfers between devices, per_device(): lax.all_to_all(asked, 'sp', split_axis=0, concat_axis=0, tiled=True)  9.44 us
    all_to_all x1, starting transfers between devices, per_device(): got = lax.all_to_all(sent, 'sp', split_axis=0, concat_axis=0, tiled=True)  5.57 us
    all_to_all x1, waiting for transfers between devices, per_device(): lax.all_to_all(asked, 'sp', split_axis=0, concat_axis=0, tiled=True)  5.48 us
    all_to_all x1, starting transfers between devices, numbers_perform(): lax.all_to_all(jnp.stack(made, 0), axis_name='mem', concat_axis=0, split_...  3.64 us
  transfers between devices with their start and end apart: 5, of which 4 were waited for; matrix products, arithmetic and copies ran while one was open for 6% of the time, Pallas kernels for 0%

profile of v1, /device:TPU:2, one launch (start us, length us, event | category | flops | bytes accessed | tf_op | source)
XLA Modules:
  0.0 157.1 jit_solution(9083427797210790335)
XLA Ops:
  6.5 0.0 copy-start.5
  6.5 0.7 broadcast_multiply_fusion.1
  7.2 0.8 convert_reduce_fusion.1
  8.1 0.1 select_reduce_fusion
  8.2 0.1 reshape.129
  8.3 0.6 pad.4
  8.9 9.4 %all-to-all-start = ((s32[32,1,128]{2,1,0:T(1,128)}), s32[32,1,128]{2,1,0:T(1,128)S(1)}, u32[]{:S(2)}, u32[]{:S(2)}) async-start(s32[32,1,128]{2,1,0:T(1,128)} %bitcast.3), calls=%async_computation | async-start | bytes 32768 | tf_op jit(solution)/shard_map/all_to_all | solution.py:40
  18.3 0.7 slice.11
  19.0 5.5 %all-to-all-done = s32[32,1,128]{2,1,0:T(1,128)S(1)} async-done(((s32[32,1,128]{2,1,0:T(1,128)}), s32[32,1,128]{2,1,0:T(1,128)S(1)}, u32[]{:S(2)}, u32[]{:S(2)}) %all-to-all-start) | async-done | bytes 16416 | tf_op jit(solution)/shard_map/all_to_all | solution.py:40
  24.5 0.6 broadcast_in_dim.19
  25.2 13.3 %all-to-all-start.2 = ((bf16[16,16,128]{2,1,0:T(8,128)(2,1)}), bf16[16,16,128]{2,1,0:T(8,128)(2,1)S(1)}, u32[]{:S(2)}, u32[]{:S(2)}) async-start(bf16[16,16,128]{2,1,0:T(8,128)(2,1)} %broadcast_in_dim.19), calls=%async_computation.2 | async-start | bytes 131072 | tf_op jit(solution)/shard_map/all_to_all | solution.py:47
  38.5 0.8 slice.9
  39.3 0.1 reshape.130
  39.4 11.7 %all-to-all-done.2 = bf16[16,16,128]{2,1,0:T(8,128)(2,1)S(1)} async-done(((bf16[16,16,128]{2,1,0:T(8,128)(2,1)}), bf16[16,16,128]{2,1,0:T(8,128)(2,1)S(1)}, u32[]{:S(2)}, u32[]{:S(2)}) %all-to-all-start.2) | async-done | bytes 65568 | tf_op jit(solution)/shard_map/all_to_all | solution.py:47
  51.1 1.1 stack.2
  52.2 3.6 %all-to-all-start.1 = ((bf16[16,16,1920]{2,1,0:T(8,128)(2,1)}), bf16[16,16,1920]{2,1,0:T(8,128)(2,1)S(1)}, u32[]{:S(2)}, u32[]{:S(2)}) async-start(bf16[16,16,1920]{2,1,0:T(8,128)(2,1)} %stack.2), calls=%async_computation.1 | async-start | bytes 1966080 | tf_op jit(solution)/shard_map/all_to_all | solution.py:14
  55.8 0.0 all-gather.2.cloned.1.call-start
  55.9 0.7 all-gather.2.cloned.1.call-update
  56.6 0.0 copy-done.5
  56.6 0.1 bitcast_sqrt_fusion
  56.7 0.1 broadcast_bitcast_fusion
  56.7 50.8 %all-to-all-done.1 = bf16[16,16,1920]{2,1,0:T(8,128)(2,1)S(1)} async-done(((bf16[16,16,1920]{2,1,0:T(8,128)(2,1)}), bf16[16,16,1920]{2,1,0:T(8,128)(2,1)S(1)}, u32[]{:S(2)}, u32[]{:S(2)}) %all-to-all-start.1) | async-done | bytes 983072 | tf_op jit(solution)/shard_map/all_to_all | solution.py:14
  107.6 1.5 maximum_convert_fusion
  109.1 0.0 copy-start.1
  109.1 0.0 copy-start.2
  109.1 0.0 copy-start.4
  109.1 2.0 %copy.41 = f32[256,2048]{0,1:T(8,128)S(1)} copy(f32[256,2048]{1,0:T(8,128)} %maximum_convert_fusion) | data formatting | bytes 4194304 | tf_op jit(solution)/shard_map/convert_element_type | solution.py:52
  111.1 0.2 fusion.15
  111.3 0.0 copy-done.1
  111.3 0.0 copy-done.2
  111.3 0.0 copy-done.4
  111.3 0.5 convolution_convert_fusion.2
  111.8 0.4 convolution_convert_fusion
  112.2 1.3 copy.45
  113.5 0.0 copy-start.3
  113.5 5.6 %all-to-all-start.3 = ((bf16[32,48,256]{2,1,0:T(8,128)(2,1)}), bf16[32,48,256]{2,1,0:T(8,128)(2,1)S(1)}, u32[]{:S(2)}, u32[]{:S(2)}) async-start(bf16[32,48,256]{2,1,0:T(8,128)(2,1)} %bitcast.11), calls=%async_computation.3 | async-start | bytes 1572864 | tf_op jit(solution)/shard_map/all_to_all | solution.py:67
  119.1 27.3 %all-gather.2.cloned.1.call-done = bf16[256,4096]{1,0:T(8,128)(2,1)} async-done(((bf16[16,4096]{1,0:T(8,128)(2,1)}), bf16[256,4096]{1,0:T(8,128)(2,1)}) %all-gather.2.cloned.1.call-update) | async-done | bytes 2097168 | tf_op jit(solution)/shard_map/all_gather | solution.py:32
  146.4 0.0 copy-start
  146.4 2.1 %convert_reduce_fusion = f32[4096]{0:T(1024)S(1)} fusion(bf16[256,4096]{1,0:T(8,128)(2,1)} %all-gather.2.cloned.1.call-done), kind=kLoop, calls=%fused_computation.1 | loop fusion | flops 2093056 | bytes 2113536 | tf_op jit(solution)/shard_map/reduce_sum | solution.py:70
  148.5 0.0 all-to-all-done.3
  148.5 0.0 copy-done.3
  148.5 0.5 convolution_convert_fusion.1
  149.0 0.0 copy-done
  149.0 0.6 fusion.8
  149.5 0.7 copy.73
  (3 shorter events, 0.0 us)
Async XLA Ops:
  6.5 50.0 %copy-start.5 = (f32[16]{0:T(128)S(1)}, f32[16]{0:T(128)}, u32[]{:S(2)}) copy-start(f32[16]{0:T(128)} %param.11) | copy-start | bytes 196
  8.9 15.6 %all-to-all-start = ((s32[32,1,128]{2,1,0:T(1,128)}), s32[32,1,128]{2,1,0:T(1,128)S(1)}, u32[]{:S(2)}, u32[]{:S(2)}) async-start(s32[32,1,128]{2,1,0:T(1,128)} %bitcast.3), calls=%async_computation | async-start | bytes 32768 | tf_op jit(solution)/shard_map/all_to_all | solution.py:40
  25.2 26.0 %all-to-all-start.2 = ((bf16[16,16,128]{2,1,0:T(8,128)(2,1)}), bf16[16,16,128]{2,1,0:T(8,128)(2,1)S(1)}, u32[]{:S(2)}, u32[]{:S(2)}) async-start(bf16[16,16,128]{2,1,0:T(8,128)(2,1)} %broadcast_in_dim.19), calls=%async_computation.2 | async-start | bytes 131072 | tf_op jit(solution)/shard_map/all_to_all | solution.py:47
  52.2 55.4 %all-to-all-start.1 = ((bf16[16,16,1920]{2,1,0:T(8,128)(2,1)}), bf16[16,16,1920]{2,1,0:T(8,128)(2,1)S(1)}, u32[]{:S(2)}, u32[]{:S(2)}) async-start(bf16[16,16,1920]{2,1,0:T(8,128)(2,1)} %stack.2), calls=%async_computation.1 | async-start | bytes 1966080 | tf_op jit(solution)/shard_map/all_to_all | solution.py:14
  55.8 90.6 %all-gather.2.cloned.1.call-start = ((), (), s32[]{:S(2)}) async-start(), calls=%async_computation.4 | async-start | bytes 2228224 | tf_op jit(solution)/shard_map/all_gather | solution.py:32
  109.1 2.2 %copy-start.1 = (bf16[16,2048]{1,0:T(8,128)(2,1)S(1)}, bf16[16,2048]{1,0:T(8,128)(2,1)}, u32[]{:S(2)}) copy-start(bf16[16,2048]{1,0:T(8,128)(2,1)} %param.8) | copy-start | bytes 196612
  109.1 2.2 %copy-start.2 = (bf16[16,2048]{1,0:T(8,128)(2,1)S(1)}, bf16[16,2048]{1,0:T(8,128)(2,1)}, u32[]{:S(2)}) copy-start(bf16[16,2048]{1,0:T(8,128)(2,1)} %param.10) | copy-start | bytes 196612
  109.1 2.2 %copy-start.4 = (f32[2048]{0:T(1024)S(1)}, f32[2048]{0:T(1024)}, u32[]{:S(2)}) copy-start(f32[2048]{0:T(1024)} %param.9) | copy-start | bytes 24580
  113.5 35.0 %copy-start.3 = (s32[32,64]{1,0:T(8,128)S(1)}, s32[32,64]{1,0:T(8,128)}, u32[]{:S(2)}) copy-start(s32[32,64]{1,0:T(8,128)} %param.13) | copy-start | bytes 24580
  113.5 35.0 %all-to-all-start.3 = ((bf16[32,48,256]{2,1,0:T(8,128)(2,1)}), bf16[32,48,256]{2,1,0:T(8,128)(2,1)S(1)}, u32[]{:S(2)}, u32[]{:S(2)}) async-start(bf16[32,48,256]{2,1,0:T(8,128)(2,1)} %bitcast.11), calls=%async_computation.3 | async-start | bytes 1572864 | tf_op jit(solution)/shard_map/all_to_all | solution.py:67
  146.4 2.6 %copy-start = (bf16[256,4096]{1,0:T(8,128)(2,1)S(1)}, bf16[256,4096]{1,0:T(8,128)(2,1)}, u32[]{:S(2)}) copy-start(bf16[256,4096]{1,0:T(8,128)(2,1)} %all-gather.2.cloned.1.call-done) | copy-start | bytes 6291460
Sparse Core Ops, SparseCore 0:
  58.8 87.5 all-gather.1
